TPU v7x, 512 devices: a whole 4x8x8 slice. The times are simulated.
512 devices in a mesh: dp: 64 (over x, z, core), refl: 8 (over y).
Axes of the slice: x: 4, y: 8, z: 8, core: 2. Of those that a mesh axis runs over, the one named last changes fastest.
Arguments:
- intensities: bfloat16 [2048, 16384], P('dp', 'refl'), may hold values from -12 to 12
- observed: int32 [2048, 16384], P('dp', 'refl'), may hold values 0 or 1
- qweights: bfloat16 [2048, 16384], P('dp', 'refl'), may hold values from 0.25 to 4
- ops: int32 [4, 16384], P(None, 'refl'), may hold values from 0 to 16383, as said below
- pick: int32 [64, 64], P(None, 'dp'), may hold values from 0 to 7
Outputs:
- corr: float32 [4, 2048, 256], P(None, ('dp', 'refl'))
- returned: float32 [4, 64, 64, 4, 32], P(None, 'dp', None, None, 'refl')
Inputs may be any that keep to these rules, and one draw needn't show every extreme that they name: Each row of ops is a permutation of the reflections that maps every aligned block of 2048 reflections onto itself.
All inputs are finite; a program needn't handle non-finite values. No bound on the sum of `observed` on one device may be relied on, other than what follows from the above.
Results may differ from a plain program's by a relative error of at most 0.0084.
Values may be sent and summed in bfloat16 or wider, within the bound.
A program may use at most 64 MiB of HBM per device.

v0:
```python
import jax
import jax.numpy as jnp
from jax import lax
from jax.sharding import PartitionSpec as P

SUB = 4
NOPS = 4


def gram(left, right):
    return lax.dot_general(
        left, right, (((1,), (1,)), ((), ())), preferred_element_type=jnp.float32
    )


def collect(stacked_own, blk, part_w, part_wy, part_wyy):
    first = gram(stacked_own, part_w).reshape(3, blk, -1)
    second = gram(stacked_own[: 2 * blk], part_wy).reshape(2, blk, -1)
    third = gram(stacked_own[:blk], part_wyy)[None]
    return jnp.concatenate([first, second, third], 0)


def pearson(share):
    total_w, sum_x, sum_xx = (share[:, 0], share[:, 1], share[:, 2])
    sum_y, sum_xy, sum_yy = (share[:, 3], share[:, 4], share[:, 5])
    numer = total_w * sum_xy - sum_x * sum_y
    var_x = jnp.maximum(total_w * sum_xx - sum_x * sum_x, 0.05 * total_w * sum_xx)
    var_y = jnp.maximum(total_w * sum_yy - sum_y * sum_y, 0.05 * total_w * sum_yy)
    return numer / jnp.sqrt(var_x * var_y)


def shards(intensities, observed, qweights, ops, pick):
    blk = intensities.shape[0]
    width = intensities.shape[1]
    groups = lax.axis_size("dp")
    shares = lax.axis_size("refl")
    weights = observed.astype(jnp.float32) * qweights.astype(jnp.float32)
    values = intensities.astype(jnp.float32)
    own_w = weights.astype(jnp.bfloat16)
    own_wx = (weights * values).astype(jnp.bfloat16)
    own_wxx = (weights * values * values).astype(jnp.bfloat16)
    stacked_own = jnp.concatenate([own_w, own_wx, own_wxx], 0)
    local_ops = ops - lax.axis_index("refl") * width
    request = pick[:, 0][:, None] * SUB + jnp.arange(SUB, dtype=jnp.int32)[None, :]
    send_x = intensities[request]
    send_w = own_w[request]
    got_x = lax.all_to_all(send_x, "dp", split_axis=0, concat_axis=0, tiled=True)
    got_w = lax.all_to_all(send_w, "dp", split_axis=0, concat_axis=0, tiled=True)
    count = got_x.shape[1]
    flat_x = got_x.reshape(-1, width)
    flat_w = got_w.reshape(-1, width)
    per_op = []
    for k in range(NOPS):
        perm = local_ops[k]
        moved_w = jnp.take(flat_w, perm, axis=1)
        wide_w = moved_w.astype(jnp.float32)
        wide_x = jnp.take(flat_x, perm, axis=1).astype(jnp.float32)
        moved_wy = (wide_w * wide_x).astype(jnp.bfloat16)
        moved_wyy = (wide_w * wide_x * wide_x).astype(jnp.bfloat16)
        per_op.append(collect(stacked_own, blk, moved_w, moved_wy, moved_wyy))
    stats = jnp.stack(per_op, 0)
    stats = stats.reshape(NOPS, 6, blk, groups, count)
    flat_stats = stats.reshape(NOPS, 6, blk, -1)
    rows = blk // shares
    totals = lax.psum(flat_stats, "refl")
    share = lax.dynamic_slice_in_dim(totals, lax.axis_index("refl") * rows, rows, 2)
    corr = pearson(share)
    outgoing = jnp.transpose(corr.reshape(NOPS, rows, groups, SUB), (0, 2, 3, 1))[:, :, None]
    returned = lax.all_to_all(outgoing, "dp", split_axis=1, concat_axis=2, tiled=True)
    return (corr, returned)


def solution(mesh):
    return jax.shard_map(
        shards,
        mesh=mesh,
        in_specs=(
            P("dp", "refl"),
            P("dp", "refl"),
            P("dp", "refl"),
            P(None, "refl"),
            P(None, "dp"),
        ),
        out_specs=(P(None, ("dp", "refl"), None), P(None, "dp", None, None, "refl")),
        check_vma=False,
    )
```

profile of v0, /device:TPU:1, one launch (start us, length us, event | category | flops | bytes accessed | tf_op | source)
XLA Modules:
  0.0 299.3 jit_solution(15204998179728151762)
XLA Ops:
  8.0 3.3 %gather_fusion.1 = bf16[256,2048]{1,0:T(8,128)(2,1)S(1)} fusion(bf16[32,2048]{1,0:T(8,128)(2,1)} %param.7, s32[1024]{0:T(1024)S(1)} %pad_clamp_fusion), kind=kCustom, calls=%fused_computation.9 | custom fusion | bytes 2098176 | tf_op jit(solution)/shard_map/gather | solution.py:45
  11.3 1.2 reshape.180
  12.5 15.0 %all-to-all-start.1 = ((bf16[64,4,2048]{2,1,0:T(4,128)(2,1)}), bf16[64,4,2048]{2,1,0:T(4,128)(2,1)S(1)}, u32[]{:S(2)}, u32[]{:S(2)}) async-start(bf16[64,4,2048]{2,1,0:T(4,128)(2,1)} %reshape.180), calls=%async_computation.1 | async-start | bytes 2097152 | tf_op jit(solution)/shard_map/all_to_all | solution.py:47
  27.6 1.4 gather_fusion
  29.0 1.2 reshape.172
  30.2 25.8 %all-to-all-done.1 = bf16[64,4,2048]{2,1,0:T(4,128)(2,1)S(1)} async-done(((bf16[64,4,2048]{2,1,0:T(4,128)(2,1)}), bf16[64,4,2048]{2,1,0:T(4,128)(2,1)S(1)}, u32[]{:S(2)}, u32[]{:S(2)}) %all-to-all-start.1) | async-done | bytes 1048608 | tf_op jit(solution)/shard_map/all_to_all | solution.py:47
  56.0 6.2 %all-to-all-start = ((bf16[64,4,2048]{2,1,0:T(4,128)(2,1)}), bf16[64,4,2048]{2,1,0:T(4,128)(2,1)S(1)}, u32[]{:S(2)}, u32[]{:S(2)}) async-start(bf16[64,4,2048]{2,1,0:T(4,128)(2,1)} %reshape.172), calls=%async_computation | async-start | bytes 2097152 | tf_op jit(solution)/shard_map/all_to_all | solution.py:48
  66.9 23.8 %all-to-all-done = bf16[64,4,2048]{2,1,0:T(4,128)(2,1)S(1)} async-done(((bf16[64,4,2048]{2,1,0:T(4,128)(2,1)}), bf16[64,4,2048]{2,1,0:T(4,128)(2,1)S(1)}, u32[]{:S(2)}, u32[]{:S(2)}) %all-to-all-start) | async-done | bytes 1048608 | tf_op jit(solution)/shard_map/all_to_all | solution.py:48
  91.6 9.8 %gather_fusion.7 = bf16[2048,256]{1,0:T(8,128)(2,1)} fusion(bf16[256,2048]{0,1:T(8,128)(2,1)S(1)} %copy.19, s32[2048]{0:T(1024)} %fusion.54), kind=kCustom, calls=%fused_computation.5.clone | custom fusion | bytes 2105344 | tf_op jit(solution)/shard_map/jit(_take)/gather | solution.py:57
  101.3 8.5 %gather_fusion.6 = bf16[2048,256]{1,0:T(8,128)(2,1)S(1)} fusion(bf16[256,2048]{0,1:T(8,128)(2,1)S(1)} %copy.18, s32[2048]{0:T(1024)} %fusion.54), kind=kCustom, calls=%fused_computation.4.clone | custom fusion | bytes 2105344 | tf_op jit(solution)/shard_map/jit(_take)/gather | solution.py:55
  109.8 9.7 %gather_fusion.9 = bf16[2048,256]{1,0:T(8,128)(2,1)} fusion(bf16[256,2048]{0,1:T(8,128)(2,1)S(1)} %copy.19, s32[2048]{0:T(1024)} %fusion.55), kind=kCustom, calls=%fused_computation.7.clone | custom fusion | bytes 2105344 | tf_op jit(solution)/shard_map/jit(_take)/gather | solution.py:57
  119.5 9.8 %gather_fusion.8 = bf16[2048,256]{1,0:T(8,128)(2,1)} fusion(bf16[256,2048]{0,1:T(8,128)(2,1)S(1)} %copy.18, s32[2048]{0:T(1024)} %fusion.55), kind=kCustom, calls=%fused_computation.6.clone | custom fusion | bytes 2105344 | tf_op jit(solution)/shard_map/jit(_take)/gather | solution.py:55
  129.3 2.6 convolution_bitcast_fusion.1
  132.0 1.2 fusion.12
  133.5 1.3 convolution_bitcast_fusion
  134.8 1.2 fusion.14
  136.0 1.2 fusion.30
  137.2 1.2 fusion.24
  138.3 9.0 %gather_fusion.3 = bf16[2048,256]{1,0:T(8,128)(2,1)} fusion(bf16[256,2048]{0,1:T(8,128)(2,1)S(1)} %copy.19, s32[2048]{0:T(1024)S(1)} %fusion.52), kind=kCustom, calls=%fused_computation.1.clone | custom fusion | bytes 2105344 | tf_op jit(solution)/shard_map/jit(_take)/gather | solution.py:57
  147.3 7.5 %gather_fusion.2 = bf16[2048,256]{1,0:T(8,128)(2,1)S(1)} fusion(bf16[256,2048]{0,1:T(8,128)(2,1)S(1)} %copy.18, s32[2048]{0:T(1024)S(1)} %fusion.52), kind=kCustom, calls=%fused_computation.clone | custom fusion | bytes 2105344 | tf_op jit(solution)/shard_map/jit(_take)/gather | solution.py:55
  154.9 2.6 convolution_bitcast_fusion.3
  157.5 1.3 fusion.8
  158.8 1.2 fusion.42
  159.9 7.5 %gather_fusion.5 = bf16[2048,256]{1,0:T(8,128)(2,1)S(1)} fusion(bf16[256,2048]{0,1:T(8,128)(2,1)S(1)} %copy.19, s32[2048]{0:T(1024)S(1)} %fusion.53), kind=kCustom, calls=%fused_computation.3.clone | custom fusion | bytes 2105344 | tf_op jit(solution)/shard_map/jit(_take)/gather | solution.py:57
  167.4 7.7 %gather_fusion.4 = bf16[2048,256]{1,0:T(8,128)(2,1)S(1)} fusion(bf16[256,2048]{0,1:T(8,128)(2,1)S(1)} %copy.18, s32[2048]{0:T(1024)S(1)} %fusion.53), kind=kCustom, calls=%fused_computation.2.clone | custom fusion | bytes 2105344 | tf_op jit(solution)/shard_map/jit(_take)/gather | solution.py:55
  177.6 1.0 pad_maximum_fusion
  178.6 72.0 %all-reduce.2.cloned.1.call-done = f32[4,6,32,256]{3,2,0,1:T(8,128)} async-done(((f32[4,6,32,256]{3,2,0,1:T(8,128)}), f32[4,6,32,256]{3,2,0,1:T(8,128)}) %all-reduce.2.cloned.1.call-update) | async-done | bytes 786448 | tf_op jit(solution)/shard_map/psum | solution.py:65
  250.7 1.5 fusion.50
  255.4 1.4 squeeze.43
  256.8 1.4 multiply_bitcast_fusion
  258.6 33.0 %all_to_all.22 = f32[4,64,1,4,4]{3,4,0,2,1:T(4,128)S(1)} all-to-all(f32[4,64,1,4,4]{3,4,0,2,1:T(4,128)S(1)} %copy.26), channel_id=1, replica_groups=mesh['dp'=64,'refl'=8] {'dp'}, dimensions={1} | all-to-all | bytes 32768 | tf_op jit(solution)/shard_map/all_to_all | solution.py:69
  291.5 0.9 copy.27
  (75 shorter events, 12.6 us)
Async XLA Ops:
  12.5 15.0 %copy-start = (bf16[32,2048]{1,0:T(8,128)(2,1)S(1)}, bf16[32,2048]{1,0:T(8,128)(2,1)}, u32[]{:S(2)}) copy-start(bf16[32,2048]{1,0:T(8,128)(2,1)} %param.7) | copy-start | bytes 393220
  12.5 15.0 %copy-start.5 = (s32[32,2048]{1,0:T(8,128)S(1)}, s32[32,2048]{1,0:T(8,128)}, u32[]{:S(2)}) copy-start(s32[32,2048]{1,0:T(8,128)} %param.8) | copy-start | bytes 786436
  12.5 15.0 %copy-start.6 = (bf16[32,2048]{1,0:T(8,128)(2,1)S(1)}, bf16[32,2048]{1,0:T(8,128)(2,1)}, u32[]{:S(2)}) copy-start(bf16[32,2048]{1,0:T(8,128)(2,1)} %param.9) | copy-start | bytes 393220
  12.5 43.5 %all-to-all-start.1 = ((bf16[64,4,2048]{2,1,0:T(4,128)(2,1)}), bf16[64,4,2048]{2,1,0:T(4,128)(2,1)S(1)}, u32[]{:S(2)}, u32[]{:S(2)}) async-start(bf16[64,4,2048]{2,1,0:T(4,128)(2,1)} %reshape.180), calls=%async_computation.1 | async-start | bytes 2097152 | tf_op jit(solution)/shard_map/all_to_all | solution.py:47
  29.0 1.2 copy-start.16
  56.0 34.7 %all-to-all-start = ((bf16[64,4,2048]{2,1,0:T(4,128)(2,1)}), bf16[64,4,2048]{2,1,0:T(4,128)(2,1)S(1)}, u32[]{:S(2)}, u32[]{:S(2)}) async-start(bf16[64,4,2048]{2,1,0:T(4,128)(2,1)} %reshape.172), calls=%async_computation | async-start | bytes 2097152 | tf_op jit(solution)/shard_map/all_to_all | solution.py:48
  62.2 188.4 %all-reduce.2.cloned.1.call-start = ((), (), s32[]{:S(2)}) async-start(), calls=%async_computation.3 | async-start | bytes 1572864 | tf_op jit(solution)/shard_map/psum | solution.py:65
  129.3 2.6 copy-start.2
  129.3 2.6 copy-start.20
  132.0 1.3 copy-start.1
  132.0 1.5 copy-start.3
  132.0 1.5 copy-start.19
  154.8 2.7 copy-start.4
  154.9 2.7 copy-start.18
  167.4 7.7 %copy-start.17 = (pred[2048]{0:T(1024)(128)(4,1)S(1)}, pred[2048]{0:T(1024)(128)(4,1)}, u32[]{:S(2)}) copy-start(pred[2048]{0:T(1024)(128)(4,1)} %compare_and_fusion.2) | copy-start | bytes 6148
  176.5 0.9 copy-start.7
  176.5 0.9 copy-start.8
  176.5 0.9 copy-start.10
  176.5 0.9 copy-start.11
  176.5 0.9 copy-start.13
  176.5 0.9 copy-start.14
  176.5 1.0 copy-start.9
  176.6 1.0 copy-start.12
  176.6 1.0 copy-start.15
Sparse Core Ops, SparseCore 0:
  178.8 71.8 all-reduce.1
where the time goes:
time: 301 us; the launch traced here: 299 us
  waiting for transfers between devices  122 us (41%)
  local copies, waits for them, and re-layouts  84.9 us (28%)
  blocking collectives  33 us (11%)
  starting transfers between devices  21.4 us (7%)
  matrix products  15.6 us (5%)
  between operations  14.4 us (5%)
  other arithmetic  8.37 us (3%)
    psum x1, waiting for transfers between devices, shards(): totals = lax.psum(flat_stats, 'refl')  72 us
    gather x4, local copies, waits for them, and re-layouts, shards(): wide_x = jnp.take(flat_x, perm, axis=1).astype(jnp.float32)  36 us
    gather x4, local copies, waits for them, and re-layouts, shards(): moved_w = jnp.take(flat_w, perm, axis=1)  33.5 us
    all_to_all x1, blocking collectives, shards(): lax.all_to_all(outgoing, 'dp', split_axis=1, concat_axis=2, tiled=True)  33 us
    all_to_all x1, waiting for transfers between devices, shards(): lax.all_to_all(send_x, 'dp', split_axis=0, concat_axis=0, tiled=True)  25.8 us
    all_to_all x1, waiting for transfers between devices, shards(): lax.all_to_all(send_w, 'dp', split_axis=0, concat_axis=0, tiled=True)  23.8 us
    dot_general x12, matrix products, gram(): lax.dot_general(left, right, (((1,), (1,)), ((), ())), preferred_element_...  15.6 us
    all_to_all x1, starting transfers between devices, shards(): lax.all_to_all(send_x, 'dp', split_axis=0, concat_axis=0, tiled=True)  15 us
  transfers between devices with their start and end apart: 3, of which 3 were waited for; matrix products, arithmetic and copies ran while one was open for 2% of the time, Pallas kernels for 0%

commit v1 on v0

--- a/solution.py
+++ b/solution.py
@@ -62,7 +62,9 @@
     stats = stats.reshape(NOPS, 6, blk, groups, count)
     flat_stats = stats.reshape(NOPS, 6, blk, -1)
     rows = blk // shares
-    totals = lax.psum(flat_stats, "refl")
+    totals = flat_stats
+    for hop in (1, 2, 4):
+        totals = totals + lax.ppermute(totals, "refl", [(dev, dev ^ hop) for dev in range(8)])
     share = lax.dynamic_slice_in_dim(totals, lax.axis_index("refl") * rows, rows, 2)
     corr = pearson(share)
     outgoing = jnp.transpose(corr.reshape(NOPS, rows, groups, SUB), (0, 2, 3, 1))[:, :, None]

time: 301 us -> 307 us (1.020)
  starting transfers between devices: 21.4 us -> 37.1 us
  waiting for transfers between devices: 122 us -> 136 us
  between operations: 14.4 us -> 1.09 us
  blocking collectives: 33 us -> 24.5 us
    ppermute x0 -> x3, waiting for transfers between devices: none -> 85.7 us  [shards(): lax.ppermute(totals, 'refl', [(dev, dev ^ hop) for dev in range(8)])]
    psum x1 -> x0, waiting for transfers between devices: 72 us -> none  [shards(): totals = lax.psum(flat_stats, 'refl')]
    ppermute x0 -> x3, starting transfers between devices: none -> 16 us  [shards(): lax.ppermute(totals, 'refl', [(dev, dev ^ hop) for dev in range(8)])]
    all_to_all x1, blocking collectives: 33 us -> 24.5 us  [shards(): lax.all_to_all(outgoing, 'dp', split_axis=1, concat_axis=2, tiled=True)]
  transfers between devices with their start and end apart: 3 -> 5, of which waited for: 3 -> 5; matrix products, arithmetic and copies ran while one was open for 2% -> 2% of each run, Pallas kernels for 0% -> 0%
where the time goes in v1:
time: 307 us; the launch traced here: 305 us
  waiting for transfers between devices  136 us (44%)
  local copies, waits for them, and re-layouts  84.6 us (28%)
  starting transfers between devices  37.1 us (12%)
  blocking collectives  24.5 us (8%)
  matrix products  15.5 us (5%)
  other arithmetic  6.96 us (2%)
    ppermute x3, waiting for transfers between devices, shards(): lax.ppermute(totals, 'refl', [(dev, dev ^ hop) for dev in range(8)])  85.7 us
    gather x4, local copies, waits for them, and re-layouts, shards(): wide_x = jnp.take(flat_x, perm, axis=1).astype(jnp.float32)  35.9 us
    gather x4, local copies, waits for them, and re-layouts, shards(): moved_w = jnp.take(flat_w, perm, axis=1)  33.2 us
    all_to_all x1, waiting for transfers between devices, shards(): lax.all_to_all(send_x, 'dp', split_axis=0, concat_axis=0, tiled=True)  25.8 us
    all_to_all x1, blocking collectives, shards(): lax.all_to_all(outgoing, 'dp', split_axis=1, concat_axis=2, tiled=True)  24.5 us
    all_to_all x1, waiting for transfers between devices, shards(): lax.all_to_all(send_w, 'dp', split_axis=0, concat_axis=0, tiled=True)  24.1 us
    ppermute x3, starting transfers between devices, shards(): lax.ppermute(totals, 'refl', [(dev, dev ^ hop) for dev in range(8)])  16 us
    dot_general x12, matrix products, gram(): lax.dot_general(left, right, (((1,), (1,)), ((), ())), preferred_element_...  15.5 us
  transfers between devices with their start and end apart: 5, of which 5 were waited for; matrix products, arithmetic and copies ran while one was open for 2% of the time, Pallas kernels for 0%

profile of v1, /device:TPU:1, one launch (start us, length us, event | category | flops | bytes accessed | tf_op | source)
XLA Modules:
  0.0 305.4 jit_solution(13412617419979126282)
XLA Ops:
  1.5 3.3 %gather_fusion.1 = bf16[256,2048]{1,0:T(8,128)(2,1)S(1)} fusion(bf16[32,2048]{1,0:T(8,128)(2,1)} %param.7, s32[1024]{0:T(1024)S(1)} %pad_clamp_fusion), kind=kCustom, calls=%fused_computation.9 | custom fusion | bytes 2098176 | tf_op jit(solution)/shard_map/gather | solution.py:45
  4.8 1.2 reshape.180
  6.0 15.0 %all-to-all-start.1 = ((bf16[64,4,2048]{2,1,0:T(4,128)(2,1)}), bf16[64,4,2048]{2,1,0:T(4,128)(2,1)S(1)}, u32[]{:S(2)}, u32[]{:S(2)}) async-start(bf16[64,4,2048]{2,1,0:T(4,128)(2,1)} %reshape.180), calls=%async_computation.1 | async-start | bytes 2097152 | tf_op jit(solution)/shard_map/all_to_all | solution.py:47
  21.1 1.4 gather_fusion
  22.5 1.2 reshape.172
  23.7 25.8 %all-to-all-done.1 = bf16[64,4,2048]{2,1,0:T(4,128)(2,1)S(1)} async-done(((bf16[64,4,2048]{2,1,0:T(4,128)(2,1)}), bf16[64,4,2048]{2,1,0:T(4,128)(2,1)S(1)}, u32[]{:S(2)}, u32[]{:S(2)}) %all-to-all-start.1) | async-done | bytes 1048608 | tf_op jit(solution)/shard_map/all_to_all | solution.py:47
  49.5 6.2 %all-to-all-start = ((bf16[64,4,2048]{2,1,0:T(4,128)(2,1)}), bf16[64,4,2048]{2,1,0:T(4,128)(2,1)S(1)}, u32[]{:S(2)}, u32[]{:S(2)}) async-start(bf16[64,4,2048]{2,1,0:T(4,128)(2,1)} %reshape.172), calls=%async_computation | async-start | bytes 2097152 | tf_op jit(solution)/shard_map/all_to_all | solution.py:48
  60.1 24.1 %all-to-all-done = bf16[64,4,2048]{2,1,0:T(4,128)(2,1)S(1)} async-done(((bf16[64,4,2048]{2,1,0:T(4,128)(2,1)}), bf16[64,4,2048]{2,1,0:T(4,128)(2,1)S(1)}, u32[]{:S(2)}, u32[]{:S(2)}) %all-to-all-start) | async-done | bytes 1048608 | tf_op jit(solution)/shard_map/all_to_all | solution.py:48
  85.0 9.7 %gather_fusion.7 = bf16[2048,256]{1,0:T(8,128)(2,1)} fusion(bf16[256,2048]{0,1:T(8,128)(2,1)S(1)} %copy.19, s32[2048]{0:T(1024)} %fusion.54), kind=kCustom, calls=%fused_computation.5.clone | custom fusion | bytes 2105344 | tf_op jit(solution)/shard_map/jit(_take)/gather | solution.py:57
  94.7 8.5 %gather_fusion.6 = bf16[2048,256]{1,0:T(8,128)(2,1)S(1)} fusion(bf16[256,2048]{0,1:T(8,128)(2,1)S(1)} %copy.18, s32[2048]{0:T(1024)} %fusion.54), kind=kCustom, calls=%fused_computation.4.clone | custom fusion | bytes 2105344 | tf_op jit(solution)/shard_map/jit(_take)/gather | solution.py:55
  103.2 9.7 %gather_fusion.9 = bf16[2048,256]{1,0:T(8,128)(2,1)} fusion(bf16[256,2048]{0,1:T(8,128)(2,1)S(1)} %copy.19, s32[2048]{0:T(1024)} %fusion.55), kind=kCustom, calls=%fused_computation.7.clone | custom fusion | bytes 2105344 | tf_op jit(solution)/shard_map/jit(_take)/gather | solution.py:57
  113.0 9.7 %gather_fusion.8 = bf16[2048,256]{1,0:T(8,128)(2,1)} fusion(bf16[256,2048]{0,1:T(8,128)(2,1)S(1)} %copy.18, s32[2048]{0:T(1024)} %fusion.55), kind=kCustom, calls=%fused_computation.6.clone | custom fusion | bytes 2105344 | tf_op jit(solution)/shard_map/jit(_take)/gather | solution.py:55
  122.7 2.6 convolution_bitcast_fusion.1
  125.3 1.2 fusion.12
  126.9 1.3 convolution_bitcast_fusion
  128.1 1.2 fusion.14
  131.7 9.0 %gather_fusion.3 = bf16[2048,256]{1,0:T(8,128)(2,1)} fusion(bf16[256,2048]{0,1:T(8,128)(2,1)S(1)} %copy.19, s32[2048]{0:T(1024)S(1)} %fusion.52), kind=kCustom, calls=%fused_computation.1.clone | custom fusion | bytes 2105344 | tf_op jit(solution)/shard_map/jit(_take)/gather | solution.py:57
  140.7 7.5 %gather_fusion.2 = bf16[2048,256]{1,0:T(8,128)(2,1)S(1)} fusion(bf16[256,2048]{0,1:T(8,128)(2,1)S(1)} %copy.18, s32[2048]{0:T(1024)S(1)} %fusion.52), kind=kCustom, calls=%fused_computation.clone | custom fusion | bytes 2105344 | tf_op jit(solution)/shard_map/jit(_take)/gather | solution.py:55
  148.2 2.6 convolution_bitcast_fusion.3
  150.8 1.2 fusion.8
  152.1 1.2 fusion.42
  153.2 7.5 %gather_fusion.5 = bf16[2048,256]{1,0:T(8,128)(2,1)S(1)} fusion(bf16[256,2048]{0,1:T(8,128)(2,1)S(1)} %copy.19, s32[2048]{0:T(1024)S(1)} %fusion.53), kind=kCustom, calls=%fused_computation.3.clone | custom fusion | bytes 2105344 | tf_op jit(solution)/shard_map/jit(_take)/gather | solution.py:57
  160.7 7.5 %gather_fusion.4 = bf16[2048,256]{1,0:T(8,128)(2,1)S(1)} fusion(bf16[256,2048]{0,1:T(8,128)(2,1)S(1)} %copy.18, s32[2048]{0:T(1024)S(1)} %fusion.53), kind=kCustom, calls=%fused_computation.2.clone | custom fusion | bytes 2105344 | tf_op jit(solution)/shard_map/jit(_take)/gather | solution.py:55
  170.8 3.2 %collective-permute-start = (f32[4,6,32,256]{3,2,0,1:T(8,128)S(1)}, f32[4,6,32,256]{3,2,0,1:T(8,128)S(1)}, u32[]{:S(2)}, u32[]{:S(2)}) collective-permute-start(f32[4,6,32,256]{3,2,0,1:T(8,128)S(1)} %pad_maximum_fusion), channel_id=1, source_target_pairs={{0,1},{1,0},{2,3},{3,2},{4,5},{5,4},{6,7},{7,6},{8,9},{9,8},{10,11... | collective-permute-start | bytes 2359304 | tf_op jit(solution)/shard_map/ppermute | solution.py:67
  174.0 17.7 %collective-permute-done = f32[4,6,32,256]{3,2,0,1:T(8,128)S(1)} collective-permute-done((f32[4,6,32,256]{3,2,0,1:T(8,128)S(1)}, f32[4,6,32,256]{3,2,0,1:T(8,128)S(1)}, u32[]{:S(2)}, u32[]{:S(2)}) %collective-permute-start) | collective-permute-done | bytes 786464 | tf_op jit(solution)/shard_map/ppermute | solution.py:67
  191.8 4.2 %collective-permute-start.1 = (f32[4,6,32,256]{3,2,0,1:T(8,128)S(1)}, f32[4,6,32,256]{3,2,0,1:T(8,128)S(1)}, u32[]{:S(2)}, u32[]{:S(2)}) collective-permute-start(f32[4,6,32,256]{3,2,0,1:T(8,128)S(1)} %fusion.64), channel_id=1, source_target_pairs={{0,2},{1,3},{2,0},{3,1},{4,6},{5,7},{6,4},{7,5},{8,10},{9,11},{10,... | collective-permute-start | bytes 2359304 | tf_op jit(solution)/shard_map/ppermute | solution.py:67
  196.0 33.9 %collective-permute-done.1 = f32[4,6,32,256]{3,2,0,1:T(8,128)S(1)} collective-permute-done((f32[4,6,32,256]{3,2,0,1:T(8,128)S(1)}, f32[4,6,32,256]{3,2,0,1:T(8,128)S(1)}, u32[]{:S(2)}, u32[]{:S(2)}) %collective-permute-start.1) | collective-permute-done | bytes 786464 | tf_op jit(solution)/shard_map/ppermute | solution.py:67
  230.1 8.6 %collective-permute-start.2 = (f32[4,6,32,256]{3,2,0,1:T(8,128)S(1)}, f32[4,6,32,256]{3,2,0,1:T(8,128)S(1)}, u32[]{:S(2)}, u32[]{:S(2)}) collective-permute-start(f32[4,6,32,256]{3,2,0,1:T(8,128)S(1)} %fusion.71), channel_id=1, source_target_pairs={{0,4},{1,5},{2,6},{3,7},{4,0},{5,1},{6,2},{7,3},{8,12},{9,13},{10,... | collective-permute-start | bytes 2359304 | tf_op jit(solution)/shard_map/ppermute | solution.py:67
  238.7 34.1 %collective-permute-done.2 = f32[4,6,32,256]{3,2,0,1:T(8,128)S(1)} collective-permute-done((f32[4,6,32,256]{3,2,0,1:T(8,128)S(1)}, f32[4,6,32,256]{3,2,0,1:T(8,128)S(1)}, u32[]{:S(2)}, u32[]{:S(2)}) %collective-permute-start.2) | collective-permute-done | bytes 786464 | tf_op jit(solution)/shard_map/ppermute | solution.py:67
  276.8 1.3 squeeze.43
  278.2 1.4 multiply_bitcast_fusion
  279.9 24.5 %all_to_all.22 = f32[4,64,1,4,4]{3,4,0,2,1:T(4,128)S(1)} all-to-all(f32[4,64,1,4,4]{3,4,0,2,1:T(4,128)S(1)} %copy.26), channel_id=1, replica_groups=mesh['dp'=64,'refl'=8] {'dp'}, dimensions={1} | all-to-all | bytes 32768 | tf_op jit(solution)/shard_map/all_to_all | solution.py:71
  (82 shorter events, 16.7 us)
Async XLA Ops:
  6.0 15.0 %copy-start = (bf16[32,2048]{1,0:T(8,128)(2,1)S(1)}, bf16[32,2048]{1,0:T(8,128)(2,1)}, u32[]{:S(2)}) copy-start(bf16[32,2048]{1,0:T(8,128)(2,1)} %param.7) | copy-start | bytes 393220
  6.0 15.0 %copy-start.5 = (s32[32,2048]{1,0:T(8,128)S(1)}, s32[32,2048]{1,0:T(8,128)}, u32[]{:S(2)}) copy-start(s32[32,2048]{1,0:T(8,128)} %param.8) | copy-start | bytes 786436
  6.0 15.0 %copy-start.6 = (bf16[32,2048]{1,0:T(8,128)(2,1)S(1)}, bf16[32,2048]{1,0:T(8,128)(2,1)}, u32[]{:S(2)}) copy-start(bf16[32,2048]{1,0:T(8,128)(2,1)} %param.9) | copy-start | bytes 393220
  6.0 43.5 %all-to-all-start.1 = ((bf16[64,4,2048]{2,1,0:T(4,128)(2,1)}), bf16[64,4,2048]{2,1,0:T(4,128)(2,1)S(1)}, u32[]{:S(2)}, u32[]{:S(2)}) async-start(bf16[64,4,2048]{2,1,0:T(4,128)(2,1)} %reshape.180), calls=%async_computation.1 | async-start | bytes 2097152 | tf_op jit(solution)/shard_map/all_to_all | solution.py:47
  22.4 1.2 copy-start.16
  49.5 34.7 %all-to-all-start = ((bf16[64,4,2048]{2,1,0:T(4,128)(2,1)}), bf16[64,4,2048]{2,1,0:T(4,128)(2,1)S(1)}, u32[]{:S(2)}, u32[]{:S(2)}) async-start(bf16[64,4,2048]{2,1,0:T(4,128)(2,1)} %reshape.172), calls=%async_computation | async-start | bytes 2097152 | tf_op jit(solution)/shard_map/all_to_all | solution.py:48
  122.7 2.6 copy-start.2
  122.7 2.6 copy-start.20
  125.3 1.3 copy-start.1
  125.3 1.5 copy-start.3
  125.3 1.5 copy-start.19
  148.2 2.6 copy-start.4
  148.2 2.6 copy-start.18
  160.7 7.5 %copy-start.17 = (pred[2048]{0:T(1024)(128)(4,1)S(1)}, pred[2048]{0:T(1024)(128)(4,1)}, u32[]{:S(2)}) copy-start(pred[2048]{0:T(1024)(128)(4,1)} %compare_and_fusion.2) | copy-start | bytes 6148
  169.6 0.9 copy-start.7
  169.6 0.9 copy-start.8
  169.6 0.9 copy-start.10
  169.6 0.9 copy-start.11
  169.6 0.9 copy-start.13
  169.6 0.9 copy-start.14
  169.6 1.0 copy-start.9
  169.6 1.0 copy-start.12
  169.6 1.0 copy-start.15
  170.8 20.9 %collective-permute-start = (f32[4,6,32,256]{3,2,0,1:T(8,128)S(1)}, f32[4,6,32,256]{3,2,0,1:T(8,128)S(1)}, u32[]{:S(2)}, u32[]{:S(2)}) collective-permute-start(f32[4,6,32,256]{3,2,0,1:T(8,128)S(1)} %pad_maximum_fusion), channel_id=1, source_target_pairs={{0,1},{1,0},{2,3},{3,2},{4,5},{5,4},{6,7},{7,6},{8,9},{9,8},{10,11... | collective-permute-start | bytes 2359304 | tf_op jit(solution)/shard_map/ppermute | solution.py:67
  191.8 38.1 %collective-permute-start.1 = (f32[4,6,32,256]{3,2,0,1:T(8,128)S(1)}, f32[4,6,32,256]{3,2,0,1:T(8,128)S(1)}, u32[]{:S(2)}, u32[]{:S(2)}) collective-permute-start(f32[4,6,32,256]{3,2,0,1:T(8,128)S(1)} %fusion.64), channel_id=1, source_target_pairs={{0,2},{1,3},{2,0},{3,1},{4,6},{5,7},{6,4},{7,5},{8,10},{9,11},{10,... | collective-permute-start | bytes 2359304 | tf_op jit(solution)/shard_map/ppermute | solution.py:67
  230.1 42.7 %collective-permute-start.2 = (f32[4,6,32,256]{3,2,0,1:T(8,128)S(1)}, f32[4,6,32,256]{3,2,0,1:T(8,128)S(1)}, u32[]{:S(2)}, u32[]{:S(2)}) collective-permute-start(f32[4,6,32,256]{3,2,0,1:T(8,128)S(1)} %fusion.71), channel_id=1, source_target_pairs={{0,4},{1,5},{2,6},{3,7},{4,0},{5,1},{6,2},{7,3},{8,12},{9,13},{10,... | collective-permute-start | bytes 2359304 | tf_op jit(solution)/shard_map/ppermute | solution.py:67
